TPU v7x, 32 devices: a whole 2x2x4 slice. The times are simulated.
32 devices in a mesh: wa: 4 (over z), ha: 8 (over y, x, core).
Axes of the slice: x: 2, y: 2, z: 4, core: 2. Of those that a mesh axis runs over, the one named last changes fastest.
Arguments:
- tokens: bfloat16 [1024, 16384], P('ha', 'wa'), may hold values from -6 to 6
- gain_attn: bfloat16 [16384], P('wa'), may hold values from 0.25 to 1.75
- w_query: bfloat16 [16384, 16384], P('wa', 'ha'), may hold values from -0.046875 to 0.046875, as said below
- w_key: bfloat16 [16384, 1024], P('wa'), may hold values from -1.171875 to 1.171875, as said below
- w_value: bfloat16 [16384, 1024], P('wa'), may hold values from -0.046875 to 0.046875
- w_out: bfloat16 [16384, 16384], P('ha', 'wa'), may hold values from -0.1875 to 0.1875
- gain_ffn: bfloat16 [16384], P('wa'), may hold values from 0.25 to 1.75
- segment_ids: int32 [1024], replicated, may hold values from 0 to 31, never falling along the last dimension, each value on 1 to 256 neighbouring positions
Outputs:
- residual_out: bfloat16 [1024, 16384], P('ha', 'wa')
- ffn_input: bfloat16 [1024, 16384], P('ha', 'wa')
Inputs may be any that keep to these rules, and one draw needn't show every extreme that they name: `w_query`: entries scaled by 16384 ** -0.5. `w_key`: entries scaled by 16384 ** -0.5. `segment_ids`: segment ids never fall along the tokens; each prompt has 1 to 256 tokens and one has exactly 256.
All inputs are finite; a program needn't handle non-finite values.
Results may differ from a plain program's by a relative error of at most 0.00675.
The roundings to bfloat16 on the way count: a program that leaves them out, or rounds other values in their place, can miss the bound.
Values may be sent and summed in bfloat16 or wider, within the bound.
A program may use at most 192 MiB of HBM per device.

v0:
```python
import jax
import jax.numpy as jnp
from jax import lax
from jax.sharding import PartitionSpec as P

KVH = 8
HD = 128
EPS = 1e-05


def rope_tables(position):
    half = HD // 2
    inverse = 500000.0 ** (-(jnp.arange(half, dtype=jnp.float32) * 2.0 / HD))
    angle = position[:, None] * inverse[None, :]
    return (jnp.cos(angle), jnp.sin(angle))


def rotate(values, cosine, sine):
    half = values.shape[-1] // 2
    first = values[..., :half]
    second = values[..., half:]
    cosine = cosine[:, None, :]
    sine = sine[:, None, :]
    return jnp.concatenate(
        [first * cosine - second * sine, second * cosine + first * sine], axis=-1
    )


def on_device(tokens, gain_attn, w_query, w_key, w_value, w_out, gain_ffn, segment_ids):
    rows_dev, width_dev = tokens.shape
    n_wa = lax.axis_size("wa")
    n_ha = lax.axis_size("ha")
    total = rows_dev * n_ha
    width = width_dev * n_wa
    head_cols = w_query.shape[1]
    heads_dev = head_cols // HD
    token_f = tokens.astype(jnp.float32)
    gain_one = gain_attn.astype(jnp.float32)
    kv_head = lax.axis_index("ha") // (n_ha // KVH)
    kv_weights = jnp.concatenate(
        [
            lax.dynamic_slice_in_dim(w_key, kv_head * HD, HD, 1),
            lax.dynamic_slice_in_dim(w_value, kv_head * HD, HD, 1),
        ],
        axis=1,
    )
    gathered = lax.all_gather(tokens, "ha", axis=0, tiled=True)
    own_sq = lax.psum(jnp.sum(token_f * token_f, axis=1), "wa")
    own_scale = lax.rsqrt(own_sq / width + EPS)
    row_scale = lax.all_gather(own_scale, "ha", axis=0, tiled=True)
    scaled = (gathered.astype(jnp.float32) * gain_one).astype(jnp.bfloat16)
    kv_part = jnp.dot(scaled, kv_weights, preferred_element_type=jnp.float32)
    kv_sum = lax.psum(kv_part, "wa")
    index_all = jnp.arange(total, dtype=jnp.int32)
    fresh = jnp.concatenate([jnp.ones((1,), dtype=bool), segment_ids[1:] != segment_ids[:-1]])
    start_all = lax.cummax(jnp.where(fresh, index_all, jnp.zeros_like(index_all)), axis=0)
    cosine, sine = rope_tables((index_all - start_all).astype(jnp.float32))
    key_plain = (kv_sum[:, :HD] * row_scale[:, None]).astype(jnp.bfloat16)
    key_plain = lax.optimization_barrier(key_plain)
    value_head = (kv_sum[:, HD:] * row_scale[:, None]).astype(jnp.bfloat16)
    key_head = rotate(key_plain.astype(jnp.float32).reshape(total, 1, HD), cosine, sine)
    key_head = key_head.reshape(total, HD).astype(jnp.bfloat16)
    q_rows = total // n_wa
    first = lax.axis_index("wa") * q_rows
    block = scaled
    query_f = lax.psum_scatter(
        jnp.dot(block, w_query, preferred_element_type=jnp.float32),
        "wa",
        scatter_dimension=0,
        tiled=True,
    )
    q_scale = lax.dynamic_slice_in_dim(row_scale, first, q_rows, 0)
    q_cos = lax.dynamic_slice_in_dim(cosine, first, q_rows, 0)
    q_sin = lax.dynamic_slice_in_dim(sine, first, q_rows, 0)
    queries = rotate(
        (query_f * q_scale[:, None]).reshape(q_rows, heads_dev, HD), q_cos, q_sin
    ).astype(jnp.bfloat16)
    q_segment = lax.dynamic_slice_in_dim(segment_ids, first, q_rows, 0)
    q_index = first + jnp.arange(q_rows, dtype=jnp.int32)
    allowed = (q_segment[:, None] == segment_ids[None, :]) & (
        index_all[None, :] <= q_index[:, None]
    )
    scores = jnp.einsum(
        "thd,sd->hts", queries, key_head, preferred_element_type=jnp.float32
    ) * HD ** (-0.5)
    scores = jnp.where(allowed[None], scores, -1e30)
    peak = jnp.max(scores, axis=-1, keepdims=True)
    expo = jnp.where(allowed[None], jnp.exp(scores - peak), 0.0)
    weights = (expo / jnp.sum(expo, axis=-1, keepdims=True)).astype(jnp.bfloat16)
    head_out = jnp.einsum("hts,sd->thd", weights, value_head, preferred_element_type=jnp.float32)
    head_out = head_out.astype(jnp.bfloat16).reshape(q_rows, head_cols)
    head_all = lax.all_gather(head_out, "wa", axis=0, tiled=True)
    block = head_all
    attended = lax.psum_scatter(
        jnp.dot(block, w_out, preferred_element_type=jnp.float32),
        "ha",
        scatter_dimension=0,
        tiled=True,
    )
    residual_out = (token_f + attended).astype(jnp.bfloat16)
    residual_f = residual_out.astype(jnp.float32)
    square_two = lax.psum(jnp.sum(residual_f * residual_f, axis=1), "wa")
    scale_two = lax.rsqrt(square_two / width + EPS)
    ffn_input = (residual_f * scale_two[:, None] * gain_ffn.astype(jnp.float32)).astype(
        jnp.bfloat16
    )
    return (residual_out, ffn_input)


def solution(mesh):
    in_specs = (
        P("ha", "wa"),
        P("wa"),
        P("wa", "ha"),
        P("wa", None),
        P("wa", None),
        P("ha", "wa"),
        P("wa"),
        P(),
    )
    out_specs = (P("ha", "wa"), P("ha", "wa"))
    return jax.shard_map(
        on_device, mesh=mesh, in_specs=in_specs, out_specs=out_specs, check_vma=False
    )
```

profile of v0, /device:TPU:0, one launch (start us, length us, event | category | flops | bytes accessed | tf_op | source)
XLA Modules:
  0.0 537.4 jit_solution(1475122119710769772)
XLA Ops:
  7.2 0.0 all-gather.4.cloned.1.call-start
  7.2 0.7 all-gather.4.cloned.1.call-update
  7.9 0.0 all-reduce.2.cloned.1.call-start
  7.9 0.7 convert_element_type.54
  8.6 1.7 constant_dynamic-slice_fusion
  10.3 56.5 %all-gather.4.cloned.1.call-done = bf16[1024,4096]{1,0:T(8,128)(2,1)} async-done(((bf16[128,4096]{1,0:T(8,128)(2,1)}), bf16[1024,4096]{1,0:T(8,128)(2,1)}) %all-gather.4.cloned.1.call-update) | async-done | bytes 8388624 | tf_op jit(solution)/shard_map/all_gather | solution.py:47
  66.9 6.7 %fusion.7 = f32[1024,256]{0,1:T(8,128)} fusion(bf16[1024,4096]{1,0:T(8,128)(2,1)} %all-gather.4.cloned.1.call-done, f32[4096]{0:T(1024)S(1)} %convert_element_type.54, bf16[4096,128]{1,0:T(8,128)(2,1)S(1)} %get-tuple-element.14, bf16[4096,128]{1,0:T(8,128)(2,1)S(1)} %get-tuple-element.15), kind=kOutput, calls=%fused_computation.11 | convolution fusion | flops 2164260864 | bytes 11550720 | tf_op jit(solution)/shard_map/dot_general | solution.py:52
  73.6 0.0 all-reduce.2.cloned.1.call-update
  73.6 0.0 reduce-scatter.3.cloned.1.call-start
  73.7 24.0 %fusion.6 = f32[1024,2048]{1,0:T(8,128)} fusion(bf16[4096,2048]{1,0:T(8,128)(2,1)} %param.10, bf16[1024,4096]{1,0:T(8,128)(2,1)} %all-gather.4.cloned.1.call-done, f32[4096]{0:T(1024)S(1)} %convert_element_type.54), kind=kOutput, calls=%fused_computation.10 | convolution fusion | flops 17192452096 | bytes 33570816 | tf_op jit(solution)/shard_map/dot_general | solution.py:67
  97.7 0.0 reduce-scatter.3.cloned.1.call-update
  97.7 0.0 all-gather.6.cloned.1.call-start
  97.8 1.1 copy-done
  98.9 0.3 fusion.8
  99.2 11.7 %psum.22 = f32[128]{0:T(128)S(1)} all-reduce(f32[128]{0:T(128)S(1)} %fusion.8), channel_id=1, replica_groups=mesh['wa'=4,'ha'=8] {'wa'}, use_global_device_ids=true, to_apply=%region_2.3 | all-reduce | flops 128 | bytes 1024 | tf_op jit(solution)/shard_map/psum | solution.py:48
  111.0 8.9 %all-gather = f32[8,1,128]{2,1,0:T(1,128)S(1)} all-gather(f32[1,1,128]{2,1,0:T(1,128)S(1)} %rsqrt_bitcast_fusion), channel_id=1, replica_groups=mesh['wa'=4,'ha'=8] {'ha'}, dimensions={0}, use_global_device_ids=true | all-gather | bytes 4608 | tf_op jit(solution)/shard_map/all_gather | solution.py:50
  119.8 0.1 dynamic_slice.21
  119.9 0.1 dynamic_slice.20
  120.0 0.1 slice_compare_fusion
  120.1 0.1 add_select_fusion
  120.1 0.3 reduce-window.9
  120.4 0.1 slice.36
  120.6 0.1 slice_reduce_fusion
  120.7 0.1 fusion.34
  120.7 0.2 broadcast_multiply_fusion
  121.0 0.5 dynamic-slice_cosine_fusion
  121.4 1.0 fusion.19
  122.4 3.3 all-reduce.2.cloned.1.call-done
  125.7 1.1 fusion.20
  126.8 1.8 fusion.27
  128.6 143.4 %reduce-scatter.3.cloned.1.call-done = f32[256,2048]{1,0:T(8,128)} async-done(((f32[1024,2048]{1,0:T(8,128)}), f32[256,2048]{1,0:T(8,128)}) %reduce-scatter.3.cloned.1.call-update) | async-done | bytes 2097168 | tf_op jit(solution)/shard_map/reduce_scatter | solution.py:66
  272.0 1.8 multiply_bitcast_fusion
  273.8 0.4 copy.33
  274.2 0.7 fusion.43
  274.9 1.4 subtract_convert_fusion
  276.2 11.8 %fusion.44 = (f32[16,256]{1,0:T(8,128)S(1)}, f32[16,256,1024]{1,2,0:T(8,128)}) fusion(pred[256,1024]{0,1:T(8,128)(4,1)} %fusion.19, bf16[1024,1,64]{0,2,1:T(8,128)(2,1)} %get-tuple-element.9, bf16[1024,1,64]{0,2,1:T(8,128)(2,1)S(1)} %get-tuple-element.8, bf16[256,16,64]{2,0,1:T(8,128)(2,1)S(1)} %get-tuple-element.5, ...), kind=kOutput, calls=%fused_computation.72 | convolution fusion | flops 1097335808 | bytes 18366464 | tf_op jit(solution)/shard_map/sub | solution.py:88
  288.0 8.2 %fusion.18 = bf16[128,16,256]{2,0,1:T(8,128)(2,1)} fusion(f32[16,256,1024]{1,2,0:T(8,128)} %get-tuple-element.13, f32[16,256]{1,0:T(8,128)S(1)} %get-tuple-element.12, f32[1024,256]{0,1:T(8,128)} %all-reduce.2.cloned.1.call-done, f32[1024]{0:T(1024)S(1)} %bitcast.55), kind=kOutput, calls=%fused_computation.28 | convolution fusion | flops 1082916864 | bytes 18370560 | tf_op jit(solution)/shard_map/hts,sd->thd/dot_general | solution.py:90
  296.3 0.0 all-gather.6.cloned.1.call-update
  296.3 0.3 reduce-scatter.5.cloned.1.call-start
  296.6 81.0 %all-gather.6.cloned.1.call-done = bf16[1024,2048]{0,1:T(8,128)(2,1)} async-done(((bf16[256,2048]{0,1:T(8,128)(2,1)}), bf16[1024,2048]{0,1:T(8,128)(2,1)}) %all-gather.6.cloned.1.call-update) | async-done | bytes 4194320 | tf_op jit(solution)/shard_map/all_gather | solution.py:92
  377.6 23.7 %fusion.45 = f32[1024,4096]{1,0:T(8,128)} fusion(bf16[1024,2048]{0,1:T(8,128)(2,1)} %all-gather.6.cloned.1.call-done, bf16[2048,4096]{1,0:T(8,128)(2,1)} %param.13), kind=kOutput, calls=%fused_computation.73 | convolution fusion | flops 17179869184 | bytes 37748736 | tf_op jit(solution)/shard_map/dot_general | solution.py:95
  401.3 0.0 reduce-scatter.5.cloned.1.call-update
  401.4 0.7 copy-done.3
  402.0 113.9 %reduce-scatter.5.cloned.1.call-done = f32[128,4096]{1,0:T(8,128)} async-done(((f32[1024,4096]{1,0:T(8,128)}), f32[128,4096]{1,0:T(8,128)}) %reduce-scatter.5.cloned.1.call-update) | async-done | bytes 2097168 | tf_op jit(solution)/shard_map/reduce_scatter | solution.py:94
  515.9 2.0 fusion.10
  517.9 0.0 copy-start.1
  517.9 11.7 %psum.23 = f32[128]{0:T(128)S(1)} all-reduce(f32[128]{0:T(128)S(1)} %get-tuple-element.2), channel_id=1, replica_groups=mesh['wa'=4,'ha'=8] {'wa'}, use_global_device_ids=true, to_apply=%region_10.11 | all-reduce | flops 128 | bytes 1024 | tf_op jit(solution)/shard_map/psum | solution.py:102
  529.6 1.3 fusion.12
  (12 shorter events, 0.1 us)
Async XLA Ops:
  7.2 59.7 %all-gather.4.cloned.1.call-start = ((), (), s32[]{:S(2)}) async-start(), calls=%async_computation.2 | async-start | bytes 9437184 | tf_op jit(solution)/shard_map/all_gather | solution.py:47
  7.9 117.8 %all-reduce.2.cloned.1.call-start = ((), (), s32[]{:S(2)}) async-start(), calls=%async_computation.3 | async-start | bytes 2097152 | tf_op jit(solution)/shard_map/psum | solution.py:53
  73.6 198.4 %reduce-scatter.3.cloned.1.call-start = ((), (), s32[]{:S(2)}) async-start(), calls=%async_computation.4 | async-start | bytes 10485760 | tf_op jit(solution)/shard_map/reduce_scatter | solution.py:66
  97.7 1.2 copy-start
  97.7 22.2 %copy-start.2 = (s32[1024]{0:T(1024)S(1)}, s32[1024]{0:T(1024)}, u32[]{:S(2)}) copy-start(s32[1024]{0:T(1024)} %param.15) | copy-start | bytes 12292
  97.7 279.9 %all-gather.6.cloned.1.call-start = ((), (), s32[]{:S(2)}) async-start(), calls=%async_computation.5 | async-start | bytes 5242880 | tf_op jit(solution)/shard_map/all_gather | solution.py:92
  296.3 219.6 %reduce-scatter.5.cloned.1.call-start = ((), (), s32[]{:S(2)}) async-start(), calls=%async_computation.6 | async-start | bytes 18874368 | tf_op jit(solution)/shard_map/reduce_scatter | solution.py:94
  401.3 0.7 copy-start.3
  517.9 13.0 %copy-start.1 = (bf16[128,4096]{1,0:T(8,128)(2,1)}, bf16[128,4096]{1,0:T(8,128)(2,1)S(1)}, u32[]{:S(2)}) copy-start(bf16[128,4096]{1,0:T(8,128)(2,1)S(1)} %get-tuple-element.3) | copy-start | bytes 3145732
Sparse Core Ops, SparseCore 0:
  9.9 56.9 all-gather.3
  73.7 51.9 all-reduce.1
  128.1 143.8 reduce-scatter.2
  296.4 81.1 all-gather.5
  401.5 114.3 reduce-scatter.4
where the time goes:
time: 538 us; the launch traced here: 537 us
  waiting for transfers between devices  399 us (74%)
  matrix products  74.5 us (14%)
  blocking collectives  32.3 us (6%)
  between operations  13.9 us (3%)
  other arithmetic  12.1 us (2%)
  local copies, waits for them, and re-layouts  5.39 us (1%)
    reduce_scatter x1, waiting for transfers between devices, on_device(): lax.psum_scatter(jnp.dot(block, w_query, preferred_element_type=jnp.float...  143 us
    reduce_scatter x1, waiting for transfers between devices, on_device(): lax.psum_scatter(jnp.dot(block, w_out, preferred_element_type=jnp.float32...  114 us
    all_gather x1, waiting for transfers between devices, on_device(): head_all = lax.all_gather(head_out, 'wa', axis=0, tiled=True)  81 us
    all_gather x1, waiting for transfers between devices, on_device(): gathered = lax.all_gather(tokens, 'ha', axis=0, tiled=True)  56.5 us
    dot_general x1, matrix products, on_device(): jnp.dot(block, w_query, preferred_element_type=jnp.float32)  24 us
    dot_general x1, matrix products, on_device(): jnp.dot(block, w_out, preferred_element_type=jnp.float32)  23.7 us
    sub x1, matrix products, on_device(): expo = jnp.where(allowed[None], jnp.exp(scores - peak), 0.0)  11.8 us
    psum x1, blocking collectives, on_device(): own_sq = lax.psum(jnp.sum(token_f * token_f, axis=1), 'wa')  11.7 us
  transfers between devices with their start and end apart: 5, of which 5 were waited for; matrix products, arithmetic and copies ran while one was open for 6% of the time, Pallas kernels for 0%

commit v1 on v0

--- a/solution.py
+++ b/solution.py
@@ -89,7 +89,12 @@
     weights = (expo / jnp.sum(expo, axis=-1, keepdims=True)).astype(jnp.bfloat16)
     head_out = jnp.einsum("hts,sd->thd", weights, value_head, preferred_element_type=jnp.float32)
     head_out = head_out.astype(jnp.bfloat16).reshape(q_rows, head_cols)
-    head_all = lax.all_gather(head_out, "wa", axis=0, tiled=True)
+    ring = [head_out]
+    for hop in range(3):
+        ring.append(lax.ppermute(ring[-1], "wa", [(dev, (dev + 1) % 4) for dev in range(4)]))
+    head_all = jnp.roll(
+        jnp.concatenate(ring[::-1], axis=0), (lax.axis_index("wa") + 1) * ring[0].shape[0], axis=0
+    )
     block = head_all
     attended = lax.psum_scatter(
         jnp.dot(block, w_out, preferred_element_type=jnp.float32),

time: 538 us -> 538 us (level)
  local copies, waits for them, and re-layouts: 5.39 us -> 11.4 us
    all_gather x1 -> x0, waiting for transfers between devices: 81 us -> none  [on_device(): head_all = lax.all_gather(head_out, 'wa', axis=0, tiled=True)]
    ppermute x0 -> x3, waiting for transfers between devices: none -> 75.7 us  [on_device(): lax.ppermute(ring[-1], 'wa', [(dev, (dev + 1) % 4) for dev in range(4)])]
    unnamed x9 -> x16, local copies, waits for them, and re-layouts: 2.22 us -> 8.1 us
  transfers between devices with their start and end apart: 5 -> 7, of which waited for: 5 -> 7; matrix products, arithmetic and copies ran while one was open for 6% -> 6% of each run, Pallas kernels for 0% -> 0%
where the time goes in v1:
time: 538 us; the launch traced here: 537 us
  waiting for transfers between devices  394 us (73%)
  matrix products  72.8 us (14%)
  blocking collectives  32.3 us (6%)
  between operations  13.9 us (3%)
  other arithmetic  12.1 us (2%)
  local copies, waits for them, and re-layouts  11.4 us (2%)
    reduce_scatter x1, waiting for transfers between devices, on_device(): lax.psum_scatter(jnp.dot(block, w_query, preferred_element_type=jnp.float...  143 us
    reduce_scatter x1, waiting for transfers between devices, on_device(): lax.psum_scatter(jnp.dot(block, w_out, preferred_element_type=jnp.float32...  114 us
    ppermute x3, waiting for transfers between devices, on_device(): lax.ppermute(ring[-1], 'wa', [(dev, (dev + 1) % 4) for dev in range(4)])  75.7 us
    all_gather x1, waiting for transfers between devices, on_device(): gathered = lax.all_gather(tokens, 'ha', axis=0, tiled=True)  56.5 us
    dot_general x1, matrix products, on_device(): jnp.dot(block, w_query, preferred_element_type=jnp.float32)  24 us
    dot_general x1, matrix products, on_device(): jnp.dot(block, w_out, preferred_element_type=jnp.float32)  22.5 us
    sub x1, matrix products, on_device(): expo = jnp.where(allowed[None], jnp.exp(scores - peak), 0.0)  12.4 us
    psum x1, blocking collectives, on_device(): own_sq = lax.psum(jnp.sum(token_f * token_f, axis=1), 'wa')  11.7 us
  transfers between devices with their start and end apart: 7, of which 7 were waited for; matrix products, arithmetic and copies ran while one was open for 6% of the time, Pallas kernels for 0%

profile of v1, /device:TPU:0, one launch (start us, length us, event | category | flops | bytes accessed | tf_op | source)
XLA Modules:
  0.0 537.3 jit_solution(8096138499343716355)
XLA Ops:
  7.2 0.7 all-gather.3.cloned.1.call-update
  7.9 0.7 convert_element_type.54
  8.6 1.7 constant_dynamic-slice_fusion
  10.3 56.5 %all-gather.3.cloned.1.call-done = bf16[1024,4096]{1,0:T(8,128)(2,1)} async-done(((bf16[128,4096]{1,0:T(8,128)(2,1)}), bf16[1024,4096]{1,0:T(8,128)(2,1)}) %all-gather.3.cloned.1.call-update) | async-done | bytes 8388624 | tf_op jit(solution)/shard_map/all_gather | solution.py:47
  66.9 6.7 %fusion.7 = f32[1024,256]{0,1:T(8,128)} fusion(bf16[1024,4096]{1,0:T(8,128)(2,1)} %all-gather.3.cloned.1.call-done, f32[4096]{0:T(1024)S(1)} %convert_element_type.54, bf16[4096,128]{1,0:T(8,128)(2,1)S(1)} %get-tuple-element.14, bf16[4096,128]{1,0:T(8,128)(2,1)S(1)} %get-tuple-element.15), kind=kOutput, calls=%fused_computation.11 | convolution fusion | flops 2164260864 | bytes 11550720 | tf_op jit(solution)/shard_map/dot_general | solution.py:52
  73.7 24.0 %fusion.6 = f32[1024,2048]{1,0:T(8,128)} fusion(bf16[4096,2048]{1,0:T(8,128)(2,1)} %param.10, bf16[1024,4096]{1,0:T(8,128)(2,1)} %all-gather.3.cloned.1.call-done, f32[4096]{0:T(1024)S(1)} %convert_element_type.54), kind=kOutput, calls=%fused_computation.10 | convolution fusion | flops 17192452096 | bytes 33570816 | tf_op jit(solution)/shard_map/dot_general | solution.py:67
  97.8 1.1 copy-done
  98.9 0.3 fusion.10
  99.2 11.7 %psum.22 = f32[128]{0:T(128)S(1)} all-reduce(f32[128]{0:T(128)S(1)} %fusion.10), channel_id=1, replica_groups=mesh['wa'=4,'ha'=8] {'wa'}, use_global_device_ids=true, to_apply=%region_2.3 | all-reduce | flops 128 | bytes 1024 | tf_op jit(solution)/shard_map/psum | solution.py:48
  111.0 8.9 %all-gather = f32[8,1,128]{2,1,0:T(1,128)S(1)} all-gather(f32[1,1,128]{2,1,0:T(1,128)S(1)} %rsqrt_bitcast_fusion), channel_id=1, replica_groups=mesh['wa'=4,'ha'=8] {'ha'}, dimensions={0}, use_global_device_ids=true | all-gather | bytes 4608 | tf_op jit(solution)/shard_map/all_gather | solution.py:50
  119.8 0.1 dynamic_slice.25
  120.0 0.1 slice_compare_fusion
  120.1 0.1 add_select_fusion
  120.1 0.3 reduce-window.9
  120.4 0.1 slice.36
  120.6 0.1 slice_reduce_fusion
  120.7 0.1 fusion.36
  120.7 0.2 broadcast_multiply_fusion
  121.0 0.5 dynamic-slice_cosine_fusion
  121.4 1.0 fusion.21
  122.4 3.3 all-reduce.2.cloned.1.call-done
  125.7 1.1 fusion.22
  126.8 1.8 fusion.29
  128.6 143.4 %reduce-scatter.3.cloned.1.call-done = f32[256,2048]{1,0:T(8,128)} async-done(((f32[1024,2048]{1,0:T(8,128)}), f32[256,2048]{1,0:T(8,128)}) %reduce-scatter.3.cloned.1.call-update) | async-done | bytes 2097168 | tf_op jit(solution)/shard_map/reduce_scatter | solution.py:66
  272.0 1.8 multiply_bitcast_fusion
  273.8 0.4 copy.33
  274.2 0.7 fusion.46
  274.9 1.4 subtract_convert_fusion
  276.2 12.4 %fusion.47 = (f32[16,256]{1,0:T(8,128)}, f32[16,256,1024]{1,2,0:T(8,128)}) fusion(pred[256,1024]{0,1:T(8,128)(4,1)} %fusion.21, bf16[1024,1,64]{0,2,1:T(8,128)(2,1)} %get-tuple-element.9, bf16[1024,1,64]{0,2,1:T(8,128)(2,1)S(1)} %get-tuple-element.8, bf16[256,16,64]{2,0,1:T(8,128)(2,1)S(1)} %get-tuple-element.5, bf16[256,16,64]{2,0,1:T(8,128)(2,1)S(1)} %get-tuple-element.4), kind=kOutput, calls=%fused_computation.83 | convolution fusion | flops 1097335808 | bytes 18366464 | tf_op jit(solution)/shard_map/sub | solution.py:88
  288.6 7.1 %fusion.20 = bf16[128,16,256]{2,0,1:T(8,128)(2,1)S(1)} fusion(f32[16,256,1024]{1,2,0:T(8,128)} %get-tuple-element.13, f32[16,256]{1,0:T(8,128)} %get-tuple-element.12, f32[1024,256]{0,1:T(8,128)} %all-reduce.2.cloned.1.call-done, f32[1024]{0:T(1024)S(1)} %bitcast.56), kind=kOutput, calls=%fused_computation.30 | convolution fusion | flops 1082916864 | bytes 18370560 | tf_op jit(solution)/shard_map/hts,sd->thd/dot_general | solution.py:90
  295.8 1.1 collective-permute-start
  296.9 25.3 %collective-permute-done = bf16[256,2048]{0,1:T(8,128)(2,1)S(1)} collective-permute-done((bf16[256,2048]{0,1:T(8,128)(2,1)S(1)}, bf16[256,2048]{0,1:T(8,128)(2,1)S(1)}, u32[]{:S(2)}, u32[]{:S(2)}) %collective-permute-start) | collective-permute-done | bytes 1048608 | tf_op jit(solution)/shard_map/ppermute | solution.py:94
  322.1 25.6 %collective-permute-done.1 = bf16[256,2048]{0,1:T(8,128)(2,1)} collective-permute-done((bf16[256,2048]{0,1:T(8,128)(2,1)S(1)}, bf16[256,2048]{0,1:T(8,128)(2,1)}, u32[]{:S(2)}, u32[]{:S(2)}) %collective-permute-start.1) | collective-permute-done | bytes 1048608 | tf_op jit(solution)/shard_map/ppermute | solution.py:94
  347.7 24.9 %collective-permute-done.2 = bf16[256,2048]{0,1:T(8,128)(2,1)} collective-permute-done((bf16[256,2048]{0,1:T(8,128)(2,1)}, bf16[256,2048]{0,1:T(8,128)(2,1)}, u32[]{:S(2)}, u32[]{:S(2)}) %collective-permute-start.2) | collective-permute-done | bytes 1048608 | tf_op jit(solution)/shard_map/ppermute | solution.py:94
  372.6 1.4 constant_dynamic-update-slice_fusion.7
  374.0 1.4 constant_dynamic-update-slice_fusion.6
  375.3 0.1 constant_dynamic-update-slice_fusion.5
  375.5 0.1 constant_dynamic-update-slice_fusion.4
  375.6 1.4 constant_dynamic-update-slice_fusion.3
  377.0 1.4 constant_dynamic-update-slice_fusion.2
  378.4 0.1 constant_dynamic-update-slice_fusion.1
  378.5 0.1 constant_dynamic-update-slice_fusion
  378.7 22.5 %fusion.8 = f32[1024,4096]{1,0:T(8,128)} fusion(bf16[2048,4096]{1,0:T(8,128)(2,1)} %param.13, bf16[2048,2048]{0,1:T(8,128)(2,1)S(1)} %constant_dynamic-update-slice_fusion, s32[]{:T(128)S(6)} %select_n.43), kind=kOutput, calls=%fused_computation.12 | convolution fusion | flops 17179869184 | bytes 37748740 | tf_op jit(solution)/shard_map/dot_general | solution.py:100
  401.2 0.7 copy-done.3
  401.9 113.8 %reduce-scatter.5.cloned.1.call-done = f32[128,4096]{1,0:T(8,128)} async-done(((f32[1024,4096]{1,0:T(8,128)}), f32[128,4096]{1,0:T(8,128)}) %reduce-scatter.5.cloned.1.call-update) | async-done | bytes 2097168 | tf_op jit(solution)/shard_map/reduce_scatter | solution.py:99
  515.7 2.0 fusion.12
  517.7 11.7 %psum.23 = f32[128]{0:T(128)S(1)} all-reduce(f32[128]{0:T(128)S(1)} %get-tuple-element.2), channel_id=1, replica_groups=mesh['wa'=4,'ha'=8] {'wa'}, use_global_device_ids=true, to_apply=%region_10.11 | all-reduce | flops 128 | bytes 1024 | tf_op jit(solution)/shard_map/psum | solution.py:107
  529.4 1.3 fusion.14
  (23 shorter events, 0.4 us)
Async XLA Ops:
  7.2 59.7 %all-gather.3.cloned.1.call-start = ((), (), s32[]{:S(2)}) async-start(), calls=%async_computation.2 | async-start | bytes 9437184 | tf_op jit(solution)/shard_map/all_gather | solution.py:47
  7.9 117.8 %all-reduce.2.cloned.1.call-start = ((), (), s32[]{:S(2)}) async-start(), calls=%async_computation.3 | async-start | bytes 2097152 | tf_op jit(solution)/shard_map/psum | solution.py:53
  73.6 198.4 %reduce-scatter.3.cloned.1.call-start = ((), (), s32[]{:S(2)}) async-start(), calls=%async_computation.4 | async-start | bytes 10485760 | tf_op jit(solution)/shard_map/reduce_scatter | solution.py:66
  97.7 1.2 copy-start
  97.7 22.2 %copy-start.2 = (s32[1024]{0:T(1024)S(1)}, s32[1024]{0:T(1024)}, u32[]{:S(2)}) copy-start(s32[1024]{0:T(1024)} %param.15) | copy-start | bytes 12292
  97.7 418.0 %reduce-scatter.5.cloned.1.call-start = ((), (), s32[]{:S(2)}) async-start(), calls=%async_computation.5 | async-start | bytes 18874368 | tf_op jit(solution)/shard_map/reduce_scatter | solution.py:99
  295.8 26.4 %collective-permute-start = (bf16[256,2048]{0,1:T(8,128)(2,1)S(1)}, bf16[256,2048]{0,1:T(8,128)(2,1)S(1)}, u32[]{:S(2)}, u32[]{:S(2)}) collective-permute-start(bf16[256,2048]{0,1:T(8,128)(2,1)S(1)} %bitcast.51), channel_id=1, source_target_pairs={{0,8},{8,16},{16,24},{24,0},{1,9},{9,17},{17,25},{25,1},{2,10},{10... | collective-permute-start | bytes 3145736 | tf_op jit(solution)/shard_map/ppermute | solution.py:94
  322.1 25.6 %collective-permute-start.1 = (bf16[256,2048]{0,1:T(8,128)(2,1)S(1)}, bf16[256,2048]{0,1:T(8,128)(2,1)}, u32[]{:S(2)}, u32[]{:S(2)}) collective-permute-start(bf16[256,2048]{0,1:T(8,128)(2,1)S(1)} %collective-permute-done), channel_id=1, source_target_pairs={{0,8},{8,16},{16,24},{24,0},{1,9},{9,17},{17,25},{25,1},{2,10},{10... | collective-permute-start | bytes 3145736 | tf_op jit(solution)/shard_map/ppermute | solution.py:94
  347.7 24.9 %collective-permute-start.2 = (bf16[256,2048]{0,1:T(8,128)(2,1)}, bf16[256,2048]{0,1:T(8,128)(2,1)}, u32[]{:S(2)}, u32[]{:S(2)}) collective-permute-start(bf16[256,2048]{0,1:T(8,128)(2,1)} %collective-permute-done.1), channel_id=1, source_target_pairs={{0,8},{8,16},{16,24},{24,0},{1,9},{9,17},{17,25},{25,1},{2,10},{10... | collective-permute-start | bytes 3145736 | tf_op jit(solution)/shard_map/ppermute | solution.py:94
  401.2 0.7 copy-start.3
  517.7 13.0 %copy-start.1 = (bf16[128,4096]{1,0:T(8,128)(2,1)}, bf16[128,4096]{1,0:T(8,128)(2,1)S(1)}, u32[]{:S(2)}) copy-start(bf16[128,4096]{1,0:T(8,128)(2,1)S(1)} %get-tuple-element.3) | copy-start | bytes 3145732
Sparse Core Ops, SparseCore 0:
  9.9 56.9 all-gather.2
  73.7 51.9 all-reduce.1
  128.1 143.8 reduce-scatter.2
  401.3 114.3 reduce-scatter.4
